TPU v7x, 128 devices: a whole 4x4x4 slice. The times are simulated.
128 devices in a mesh: corpus: 16 (over z, y), fsdp: 2 (over core), tensor: 4 (over x).
Axes of the slice: x: 4, y: 4, z: 4, core: 2. Of those that a mesh axis runs over, the one named last changes fastest.
Arguments:
- queries_in: bfloat16 [4096, 4096], P(('corpus', 'fsdp')), may hold values from -6 to 6
- head_weight: bfloat16 [4096, 4096], P('fsdp', 'tensor'), may hold values from -0.09375 to 0.09375
- passages: bfloat16 [16384, 4096], P('corpus', 'tensor'), may hold values from -0.15625 to 0.15625
- teacher: float32 [4096, 4, 32], P(('corpus', 'fsdp')), may hold values from -250 to 400
- cand_block: int32 [4096, 4], P(('corpus', 'fsdp')), may hold values from 0 to 127, all different within a row; in each aligned block of 128 rows (0 to 127, 128 to 255, ...) at most 6 rows name the same one
- cand_offset: int32 [4096, 4, 32], P(('corpus', 'fsdp')), may hold values from 0 to 127, as said below
- block_slot: int32 [128], replicated, may hold values from 0 to 127, each once
Outputs:
- kl_loss: float32 [4096], P(('corpus', 'fsdp'))
- head_grad: float32 [4096, 4096], P('fsdp', 'tensor')
Inputs may be any that keep to these rules, and one draw needn't show every extreme that they name: `cand_block`: in the rows of one device no block id appears more than 6 times, and some block id appears exactly 6 times there; the 4 ids of one query differ. `cand_offset`: the 32 offsets of one query in one block differ. `block_slot`: each storage position is taken by exactly one block.
All inputs are finite; a program needn't handle non-finite values.
Results may differ from a plain program's by a relative error of at most 0.012.
The roundings to bfloat16 on the way count: a program that leaves them out, or rounds other values in their place, can miss the bound.
Values may be sent and summed in bfloat16 or wider, within the bound.
A program may use at most 128 MiB of HBM per device.

v0:
```python
import jax
import jax.numpy as jnp
from jax import lax
from jax.sharding import PartitionSpec as P

ROWS = 128
MOSTB = 6


def on_device(queries_in, head_weight, passages, teacher, cand_block, cand_offset, block_slot):
    query_rows, model_width = queries_in.shape
    head_cols = head_weight.shape[1]
    per_query = cand_block.shape[1]
    offset_count = cand_offset.shape[2]
    total_blocks = block_slot.shape[0]
    n_corpus = lax.axis_size("corpus")
    blocks_here = passages.shape[0] // ROWS
    capacity = MOSTB
    slot_total = total_blocks * capacity
    columns = queries_in
    query = jnp.dot(
        columns,
        lax.all_gather(head_weight, "fsdp", axis=0, tiled=True),
        preferred_element_type=jnp.float32,
    ).astype(jnp.bfloat16)
    block_ids = lax.broadcasted_iota(jnp.int32, (1, total_blocks), 1)
    named = (cand_block.reshape(-1, 1) == block_ids).astype(jnp.int32)
    slot_of = jnp.sum(named * block_slot.reshape(1, -1), axis=1)
    slot_hits = (slot_of[:, None] == block_ids).astype(jnp.int32)
    slot_rank = jnp.sum((jnp.cumsum(slot_hits, axis=0) - slot_hits) * slot_hits, axis=1)
    position = slot_of * capacity + slot_rank
    query_copies = jnp.repeat(query, per_query, axis=0)
    send_queries = jnp.zeros((slot_total, head_cols), jnp.bfloat16).at[position].set(query_copies)
    send_queries = send_queries.reshape(n_corpus, blocks_here, capacity, head_cols)
    offset_rows = cand_offset.reshape(-1, offset_count)
    send_offsets = jnp.zeros((slot_total, offset_count), jnp.int32).at[position].set(offset_rows)
    send_offsets = send_offsets.reshape(n_corpus, blocks_here, capacity, offset_count)
    embedded = passages.reshape(blocks_here, ROWS, head_cols)
    scores = jnp.einsum(
        "sjmd,jrd->sjmr",
        lax.all_to_all(send_queries, "corpus", split_axis=0, concat_axis=0, tiled=True),
        embedded,
        preferred_element_type=jnp.float32,
    )
    returned_scores = lax.all_to_all(scores, "corpus", split_axis=0, concat_axis=0, tiled=True)
    picked = returned_scores.reshape(slot_total, ROWS)[position].reshape(
        query_rows, per_query, ROWS
    )
    partial_scores = jnp.take_along_axis(picked, cand_offset, axis=2)
    student = 50.0 * lax.psum(partial_scores, "tensor")
    log_student = student - jax.nn.logsumexp(student, axis=(1, 2), keepdims=True)
    log_teacher = teacher - jax.nn.logsumexp(teacher, axis=(1, 2), keepdims=True)
    prob_teacher = jnp.exp(log_teacher)
    kl_loss = jnp.sum(prob_teacher * (log_teacher - log_student), axis=(1, 2))
    dscore = (50.0 * (jnp.exp(log_student) - prob_teacher)).astype(jnp.bfloat16)
    flat_index = (position[:, None] * ROWS + offset_rows).reshape(-1)
    dense_grad = (
        jnp.zeros((slot_total * ROWS,), jnp.bfloat16).at[flat_index].set(dscore.reshape(-1))
    )
    dense_grad = dense_grad.reshape(n_corpus, blocks_here, capacity, ROWS)
    block_part = jnp.einsum(
        "sjmr,jrd->sjmd",
        lax.all_to_all(dense_grad, "corpus", split_axis=0, concat_axis=0, tiled=True),
        embedded,
        preferred_element_type=jnp.float32,
    ).astype(jnp.bfloat16)
    arrived_parts = lax.all_to_all(block_part, "corpus", split_axis=0, concat_axis=0, tiled=True)
    parts = arrived_parts.reshape(slot_total, head_cols)[position].reshape(
        query_rows, per_query, head_cols
    )
    query_grad = jnp.sum(parts.astype(jnp.float32), axis=1).astype(jnp.bfloat16)
    columns = queries_in
    grad_share = lax.psum_scatter(
        lax.dot_general(
            columns, query_grad, (((0,), (0,)), ((), ())), preferred_element_type=jnp.float32
        ),
        "fsdp",
        scatter_dimension=0,
        tiled=True,
    )
    head_grad = lax.psum(grad_share, "corpus")
    return (kl_loss, head_grad)


def solution(mesh):
    placed = (
        P(("corpus", "fsdp"), None),
        P("fsdp", "tensor"),
        P("corpus", "tensor"),
        P(("corpus", "fsdp"), None, None),
        P(("corpus", "fsdp"), None),
        P(("corpus", "fsdp"), None, None),
        P(),
    )
    return jax.shard_map(
        on_device,
        mesh=mesh,
        in_specs=placed,
        out_specs=(P(("corpus", "fsdp")), P("fsdp", "tensor")),
        check_vma=False,
    )
```

profile of v0, /device:TPU:0, one launch (start us, length us, event | category | flops | bytes accessed | tf_op | source)
XLA Modules:
  0.0 656.1 jit_solution(10483691207682673269)
XLA Ops:
  10.5 24.3 %all-gather.2.cloned.1.call-done = bf16[4096,1024]{1,0:T(8,128)(2,1)} async-done(((bf16[2048,1024]{1,0:T(8,128)(2,1)}), bf16[4096,1024]{1,0:T(8,128)(2,1)}) %all-gather.2.cloned.1.call-update) | async-done | bytes 8388624 | tf_op jit(solution)/shard_map/all_gather | solution.py:23
  34.7 4.6 convolution_convert_fusion.1
  40.8 4.5 scatter_custom_fusion
  45.3 3.7 reshape.158
  49.0 3.8 copy.62
  52.8 7.1 %all-to-all-start = ((bf16[16,8,6,1024]{3,1,2,0:T(8,128)(2,1)}), bf16[16,8,6,1024]{3,1,2,0:T(8,128)(2,1)}, u32[]{:S(2)}, u32[]{:S(2)}) async-start(bf16[16,8,6,1024]{3,1,2,0:T(8,128)(2,1)} %copy.62), calls=%async_computation | async-start | bytes 3145728 | tf_op jit(solution)/shard_map/all_to_all | solution.py:41
  60.6 24.8 %all-to-all-done = bf16[16,8,6,1024]{3,1,2,0:T(8,128)(2,1)} async-done(((bf16[16,8,6,1024]{3,1,2,0:T(8,128)(2,1)}), bf16[16,8,6,1024]{3,1,2,0:T(8,128)(2,1)}, u32[]{:S(2)}, u32[]{:S(2)}) %all-to-all-start) | async-done | bytes 1572896 | tf_op jit(solution)/shard_map/all_to_all | solution.py:41
  85.4 2.6 fusion.3
  89.0 3.6 all-to-all-start.1
  93.1 9.3 %all-to-all-done.1 = f32[16,8,6,128]{3,1,2,0:T(8,128)S(1)} async-done(((f32[16,8,6,128]{3,1,2,0:T(8,128)}), f32[16,8,6,128]{3,1,2,0:T(8,128)S(1)}, u32[]{:S(2)}, u32[]{:S(2)}) %all-to-all-start.1) | async-done | bytes 393248 | tf_op jit(solution)/shard_map/all_to_all | solution.py:45
  103.6 145.8 %gather_fusion.2 = f32[16384]{0:T(1024)S(1)} fusion(f32[128,4,128]{2,1,0:T(4,128)S(1)} %bitcast.43, s32[16384]{0:T(1024)S(1)} %reshape.184), kind=kCustom, calls=%fused_computation.2 | custom fusion | bytes 327680 | tf_op jit(solution)/shard_map/jit(take_along_axis)/gather | solution.py:49
  250.7 38.4 %all-reduce.3.cloned.1.call-done = f32[128,4,32]{0,2,1:T(8,128)} async-done(((f32[128,4,32]{0,2,1:T(8,128)}), f32[128,4,32]{0,2,1:T(8,128)}) %all-reduce.3.cloned.1.call-update) | async-done | bytes 65552 | tf_op jit(solution)/shard_map/psum | solution.py:50
  292.5 112.7 %scatter_custom_fusion.1 = bf16[98304]{0:T(1024)(128)(2,1)S(1)} fusion(s32[16384]{0:T(1024)} %bitcast.46, bf16[16384]{0:T(1024)(128)(2,1)S(1)} %reshape.202, bf16[]{:T(256)} %constant.17.clone.1), kind=kCustom, calls=%fused_computation.28 | custom fusion | bytes 197120 | tf_op jit(solution)/shard_map/scatter | solution.py:58
  405.4 15.1 %all_to_all.20 = bf16[16,8,6,128]{3,1,2,0:T(8,128)(2,1)S(1)} all-to-all(bf16[16,8,6,128]{3,1,2,0:T(8,128)(2,1)S(1)} %copy.70), channel_id=1, replica_groups=mesh['corpus'=16,'fsdp'=2,'tensor'=4] {'corpus'}, dimensions={0} | all-to-all | bytes 393216 | tf_op jit(solution)/shard_map/all_to_all | solution.py:63
  421.9 22.4 %all_to_all.21 = bf16[16,8,6,1024]{3,1,2,0:T(8,128)(2,1)S(1)} all-to-all(bf16[16,8,6,1024]{3,1,2,0:T(8,128)(2,1)S(1)} %copy.72), channel_id=1, replica_groups=mesh['corpus'=16,'fsdp'=2,'tensor'=4] {'corpus'}, dimensions={0} | all-to-all | bytes 3145728 | tf_op jit(solution)/shard_map/all_to_all | solution.py:67
  444.3 2.4 copy.73
  446.7 3.7 reshape.166
  450.5 5.1 gather_fusion.1
  455.6 2.3 reshape.167
  457.9 2.5 reduce_sum.62
  460.4 8.1 %convolution_bitcast_fusion = f32[4096,1024]{0,1:T(8,128)} fusion(bf16[128,1024]{1,0:T(8,128)(2,1)S(1)} %reduce_sum.62, bf16[128,4096]{1,0:T(8,128)(2,1)S(1)} %copy-done.2), kind=kOutput, calls=%fused_computation.5 | convolution fusion | flops 1073741824 | bytes 18087936 | tf_op jit(solution)/shard_map/dot_general | solution.py:74
  468.6 24.9 %reduce-scatter.2.cloned.1.call-done = f32[2048,1024]{0,1:T(8,128)} async-done(((f32[4096,1024]{0,1:T(8,128)}), f32[2048,1024]{0,1:T(8,128)}) %reduce-scatter.2.cloned.1.call-update) | async-done | bytes 8388624 | tf_op jit(solution)/shard_map/reduce_scatter | solution.py:73
  493.5 146.8 %all-reduce.5.cloned.1.call-done = f32[2048,1024]{0,1:T(8,128)} async-done(((f32[2048,1024]{0,1:T(8,128)}), f32[2048,1024]{0,1:T(8,128)}) %all-reduce.5.cloned.1.call-update) | async-done | bytes 8388624 | tf_op jit(solution)/shard_map/psum | solution.py:81
  640.4 9.2 %copy.74 = f32[2048,1024]{1,0:T(8,128)} copy(f32[2048,1024]{0,1:T(8,128)} %all-reduce.5.cloned.1.call-done) | data formatting | bytes 16777216
  (71 shorter events, 14.2 us)
Async XLA Ops:
  7.2 78.2 %copy-start = (bf16[1024,1024]{1,0:T(8,128)(2,1)S(1)}, bf16[1024,1024]{1,0:T(8,128)(2,1)}, u32[]{:S(2)}) copy-start(bf16[1024,1024]{1,0:T(8,128)(2,1)} %param.9) | copy-start | bytes 6291460
  7.2 0.8 copy-start.6
  7.2 1.0 copy-start.7
  7.2 2.3 copy-start.3
  7.2 27.5 %copy-start.1 = (bf16[128,4096]{1,0:T(8,128)(2,1)S(1)}, bf16[128,4096]{1,0:T(8,128)(2,1)}, u32[]{:S(2)}) copy-start(bf16[128,4096]{1,0:T(8,128)(2,1)} %param.7) | copy-start | bytes 3145732
  7.2 27.5 %all-gather.2.cloned.1.call-start = ((), (), s32[]{:S(2)}) async-start(), calls=%async_computation.5 | async-start | bytes 12582912 | tf_op jit(solution)/shard_map/all_gather | solution.py:23
  49.0 10.9 %copy-start.5 = (s32[16384,1]{0,1:T(1,128)S(1)}, s32[16384,1]{0,1:T(1,128)}, u32[]{:S(2)}) copy-start(s32[16384,1]{0,1:T(1,128)} %reshape.163) | copy-start | bytes 196612
  52.8 32.6 %all-to-all-start = ((bf16[16,8,6,1024]{3,1,2,0:T(8,128)(2,1)}), bf16[16,8,6,1024]{3,1,2,0:T(8,128)(2,1)}, u32[]{:S(2)}, u32[]{:S(2)}) async-start(bf16[16,8,6,1024]{3,1,2,0:T(8,128)(2,1)} %copy.62), calls=%async_computation | async-start | bytes 3145728 | tf_op jit(solution)/shard_map/all_to_all | solution.py:41
  85.4 7.6 %copy-start.4 = (f32[128,4,32]{0,2,1:T(8,128)S(1)}, f32[128,4,32]{0,2,1:T(8,128)}, u32[]{:S(2)}) copy-start(f32[128,4,32]{0,2,1:T(8,128)} %param.10) | copy-start | bytes 196612
  89.0 13.4 %all-to-all-start.1 = ((f32[16,8,6,128]{3,1,2,0:T(8,128)}), f32[16,8,6,128]{3,1,2,0:T(8,128)S(1)}, u32[]{:S(2)}, u32[]{:S(2)}) async-start(f32[16,8,6,128]{3,1,2,0:T(8,128)} %copy.64), calls=%async_computation.1 | async-start | bytes 786432 | tf_op jit(solution)/shard_map/all_to_all | solution.py:45
  92.6 196.5 %all-reduce.3.cloned.1.call-start = ((), (), s32[]{:S(2)}) async-start(), calls=%async_computation.6 | async-start | bytes 131072 | tf_op jit(solution)/shard_map/psum | solution.py:50
  250.4 243.1 %reduce-scatter.2.cloned.1.call-start = ((), (), s32[]{:S(2)}) async-start(), calls=%async_computation.7 | async-start | bytes 25165824 | tf_op jit(solution)/shard_map/reduce_scatter | solution.py:73
  455.6 4.9 copy-start.2
  468.5 171.8 %all-reduce.5.cloned.1.call-start = ((), (), s32[]{:S(2)}) async-start(), calls=%async_computation.8 | async-start | bytes 16777216 | tf_op jit(solution)/shard_map/psum | solution.py:81
Sparse Core Ops, SparseCore 0:
  9.7 25.0 all-gather.1
  250.6 38.4 all-reduce.2
  468.6 24.7 reduce-scatter.1
  497.0 143.3 all-reduce.4
where the time goes:
time: 657 us; the launch traced here: 656 us
  local copies, waits for them, and re-layouts  300 us (46%)
  waiting for transfers between devices  269 us (41%)
  blocking collectives  37.5 us (6%)
  matrix products  15.9 us (2%)
  between operations  14.1 us (2%)
  starting transfers between devices  11 us (2%)
  other arithmetic  7.89 us (1%)
    psum x1, waiting for transfers between devices, on_device(): head_grad = lax.psum(grad_share, 'corpus')  147 us
    gather x5, local copies, waits for them, and re-layouts, on_device(): partial_scores = jnp.take_along_axis(picked, cand_offset, axis=2)  146 us
    scatter x1, local copies, waits for them, and re-layouts, on_device(): jnp.zeros((slot_total * ROWS,), jnp.bfloat16).at[flat_index]  113 us
    psum x1, waiting for transfers between devices, on_device(): student = 50.0 * lax.psum(partial_scores, 'tensor')  38.4 us
    reduce_scatter x1, waiting for transfers between devices, on_device(): lax.psum_scatter(lax.dot_general(columns, query_grad, (((0,), (0,)), ((),...  24.9 us
    all_to_all x1, waiting for transfers between devices, on_device(): lax.all_to_all(send_queries, 'corpus', split_axis=0, concat_axis=0, tiled...  24.8 us
    all_gather x1, waiting for transfers between devices, on_device(): lax.all_gather(head_weight, 'fsdp', axis=0, tiled=True)  24.3 us
    all_to_all x1, blocking collectives, on_device(): lax.all_to_all(block_part, 'corpus', split_axis=0, concat_axis=0, tiled=T...  22.4 us
  transfers between devices with their start and end apart: 6, of which 6 were waited for; matrix products, arithmetic and copies ran while one was open for 1% of the time, Pallas kernels for 0%

commit v1 on v0

--- a/solution.py
+++ b/solution.py
@@ -78,7 +78,11 @@
         scatter_dimension=0,
         tiled=True,
     )
-    head_grad = lax.psum(grad_share, "corpus")
+    head_grad = grad_share
+    for hop in (1, 2, 4, 8):
+        head_grad = head_grad + lax.ppermute(
+            head_grad, "corpus", [(dev, dev ^ hop) for dev in range(16)]
+        )
     return (kl_loss, head_grad)
 
 

time: 657 us -> 1290 us (1.96)
  waiting for transfers between devices: 269 us -> 840 us
  other arithmetic: 7.89 us -> 55.8 us
    ppermute x0 -> x4, waiting for transfers between devices: none -> 720 us  [on_device(): lax.ppermute(head_grad, 'corpus', [(dev, dev ^ hop) for dev in range(16)])]
    psum x1 -> x0, waiting for transfers between devices: 147 us -> none  [on_device(): head_grad = lax.psum(grad_share, 'corpus')]
    add x0 -> x4, other arithmetic: none -> 47.3 us  [on_device(): head_grad + lax.ppermute(head_grad, 'corpus', [(dev, dev ^ hop) for dev i...]
  transfers between devices with their start and end apart: 6 -> 9, of which waited for: 6 -> 9; matrix products, arithmetic and copies ran while one was open for 1% -> 0% of each run, Pallas kernels for 0% -> 0%
where the time goes in v1:
time: 1290 us
  waiting for transfers between devices  840 us (65%)
  local copies, waits for them, and re-layouts  302 us (23%)
  other arithmetic  55.8 us (4%)
  blocking collectives  37.5 us (3%)
  starting transfers between devices  20.6 us (2%)
  matrix products  15.9 us (1%)
  between operations  14 us (1%)
    ppermute x4, waiting for transfers between devices, on_device(): lax.ppermute(head_grad, 'corpus', [(dev, dev ^ hop) for dev in range(16)])  720 us
    gather x5, local copies, waits for them, and re-layouts, on_device(): partial_scores = jnp.take_along_axis(picked, cand_offset, axis=2)  146 us
    scatter x1, local copies, waits for them, and re-layouts, on_device(): jnp.zeros((slot_total * ROWS,), jnp.bfloat16).at[flat_index]  113 us
    add x4, other arithmetic, on_device(): head_grad + lax.ppermute(head_grad, 'corpus', [(dev, dev ^ hop) for dev i...  47.3 us
    psum x1, waiting for transfers between devices, on_device(): student = 50.0 * lax.psum(partial_scores, 'tensor')  38.4 us
  transfers between devices with their start and end apart: 9, of which 9 were waited for; matrix products, arithmetic and copies ran while one was open for 0% of the time, Pallas kernels for 0%

profile of v1, /device:TPU:0, one launch (start us, length us, event | category | flops | bytes accessed | tf_op | source)
XLA Modules:
  0.0 1285.7 jit_solution(11756561871869770740)
XLA Ops:
  12.5 22.2 %all-gather.2.cloned.1.call-done = bf16[4096,1024]{1,0:T(8,128)(2,1)} async-done(((bf16[2048,1024]{1,0:T(8,128)(2,1)}), bf16[4096,1024]{1,0:T(8,128)(2,1)}) %all-gather.2.cloned.1.call-update) | async-done | bytes 8388624 | tf_op jit(solution)/shard_map/all_gather | solution.py:23
  34.7 4.6 convolution_convert_fusion.1
  40.8 4.5 scatter_custom_fusion
  52.8 7.1 all-to-all-start
  60.6 24.8 %all-to-all-done = bf16[16,8,6,1024]{3,1,2,0:T(8,128)(2,1)} async-done(((bf16[16,8,6,1024]{3,1,2,0:T(8,128)(2,1)}), bf16[16,8,6,1024]{3,1,2,0:T(8,128)(2,1)}, u32[]{:S(2)}, u32[]{:S(2)}) %all-to-all-start) | async-done | bytes 1572896 | tf_op jit(solution)/shard_map/all_to_all | solution.py:41
  93.0 9.3 all-to-all-done.1
  103.6 145.8 %gather_fusion.2 = f32[16384]{0:T(1024)S(1)} fusion(f32[128,4,128]{2,1,0:T(4,128)S(1)} %bitcast.43, s32[16384]{0:T(1024)S(1)} %reshape.184), kind=kCustom, calls=%fused_computation.2 | custom fusion | bytes 327680 | tf_op jit(solution)/shard_map/jit(take_along_axis)/gather | solution.py:49
  250.6 38.4 %all-reduce.2.cloned.1.call-done = f32[128,4,32]{0,2,1:T(8,128)} async-done(((f32[128,4,32]{0,2,1:T(8,128)}), f32[128,4,32]{0,2,1:T(8,128)}) %all-reduce.2.cloned.1.call-update) | async-done | bytes 65552 | tf_op jit(solution)/shard_map/psum | solution.py:50
  292.5 112.7 %scatter_custom_fusion.1 = bf16[98304]{0:T(1024)(128)(2,1)S(1)} fusion(s32[16384]{0:T(1024)} %bitcast.46, bf16[16384]{0:T(1024)(128)(2,1)S(1)} %reshape.202, bf16[]{:T(256)} %constant.17.clone.1), kind=kCustom, calls=%fused_computation.28 | custom fusion | bytes 197120 | tf_op jit(solution)/shard_map/scatter | solution.py:58
  405.3 15.1 %all_to_all.20 = bf16[16,8,6,128]{3,1,2,0:T(8,128)(2,1)S(1)} all-to-all(bf16[16,8,6,128]{3,1,2,0:T(8,128)(2,1)S(1)} %copy.70), channel_id=1, replica_groups=mesh['corpus'=16,'fsdp'=2,'tensor'=4] {'corpus'}, dimensions={0} | all-to-all | bytes 393216 | tf_op jit(solution)/shard_map/all_to_all | solution.py:63
  421.9 22.4 %all_to_all.21 = bf16[16,8,6,1024]{3,1,2,0:T(8,128)(2,1)S(1)} all-to-all(bf16[16,8,6,1024]{3,1,2,0:T(8,128)(2,1)S(1)} %copy.72), channel_id=1, replica_groups=mesh['corpus'=16,'fsdp'=2,'tensor'=4] {'corpus'}, dimensions={0} | all-to-all | bytes 3145728 | tf_op jit(solution)/shard_map/all_to_all | solution.py:67
  446.7 3.8 reshape.166
  450.5 5.1 gather_fusion.1
  460.4 8.1 convolution_bitcast_fusion
  468.5 25.0 %reduce-scatter.2.cloned.1.call-done = f32[2048,1024]{0,1:T(8,128)} async-done(((f32[4096,1024]{0,1:T(8,128)}), f32[2048,1024]{0,1:T(8,128)}) %reduce-scatter.2.cloned.1.call-update) | async-done | bytes 8388624 | tf_op jit(solution)/shard_map/reduce_scatter | solution.py:73
  495.1 181.2 %collective-permute-done = f32[2048,1024]{0,1:T(8,128)} collective-permute-done((f32[2048,1024]{0,1:T(8,128)}, f32[2048,1024]{0,1:T(8,128)}, u32[]{:S(2)}, u32[]{:S(2)}) %collective-permute-start) | collective-permute-done | bytes 8388640 | tf_op jit(solution)/shard_map/ppermute | solution.py:83
  676.3 11.9 add.111
  691.3 180.3 %collective-permute-done.1 = f32[2048,1024]{0,1:T(8,128)} collective-permute-done((f32[2048,1024]{0,1:T(8,128)}, f32[2048,1024]{0,1:T(8,128)}, u32[]{:S(2)}, u32[]{:S(2)}) %collective-permute-start.1) | collective-permute-done | bytes 8388640 | tf_op jit(solution)/shard_map/ppermute | solution.py:83
  871.6 11.9 add.112
  885.2 179.4 %collective-permute-done.2 = f32[2048,1024]{0,1:T(8,128)} collective-permute-done((f32[2048,1024]{0,1:T(8,128)}, f32[2048,1024]{0,1:T(8,128)}, u32[]{:S(2)}, u32[]{:S(2)}) %collective-permute-start.2) | collective-permute-done | bytes 8388640 | tf_op jit(solution)/shard_map/ppermute | solution.py:83
  1064.6 11.9 add.113
  1079.7 178.5 %collective-permute-done.3 = f32[2048,1024]{0,1:T(8,128)} collective-permute-done((f32[2048,1024]{0,1:T(8,128)}, f32[2048,1024]{0,1:T(8,128)}, u32[]{:S(2)}, u32[]{:S(2)}) %collective-permute-start.3) | collective-permute-done | bytes 8388640 | tf_op jit(solution)/shard_map/ppermute | solution.py:83
  1258.3 11.7 add.114
  1269.9 9.2 copy.74
  (76 shorter events, 46.7 us)
Async XLA Ops:
  7.2 78.2 %copy-start = (bf16[1024,1024]{1,0:T(8,128)(2,1)S(1)}, bf16[1024,1024]{1,0:T(8,128)(2,1)}, u32[]{:S(2)}) copy-start(bf16[1024,1024]{1,0:T(8,128)(2,1)} %param.9) | copy-start | bytes 6291460
  7.2 27.5 %copy-start.1 = (bf16[128,4096]{1,0:T(8,128)(2,1)S(1)}, bf16[128,4096]{1,0:T(8,128)(2,1)}, u32[]{:S(2)}) copy-start(bf16[128,4096]{1,0:T(8,128)(2,1)} %param.7) | copy-start | bytes 3145732
  7.2 27.5 %all-gather.2.cloned.1.call-start = ((), (), s32[]{:S(2)}) async-start(), calls=%async_computation.5 | async-start | bytes 12582912 | tf_op jit(solution)/shard_map/all_gather | solution.py:23
  39.3 20.5 %copy-start.5 = (s32[16384,1]{0,1:T(1,128)S(1)}, s32[16384,1]{0,1:T(1,128)}, u32[]{:S(2)}) copy-start(s32[16384,1]{0,1:T(1,128)} %reshape.163) | copy-start | bytes 196612
  39.4 21.3 %copy-start.3 = (s32[128,4,32]{0,2,1:T(8,128)S(1)}, s32[128,4,32]{0,2,1:T(8,128)}, u32[]{:S(2)}) copy-start(s32[128,4,32]{0,2,1:T(8,128)} %param.12) | copy-start | bytes 196612
  45.3 47.6 %copy-start.4 = (f32[128,4,32]{0,2,1:T(8,128)S(1)}, f32[128,4,32]{0,2,1:T(8,128)}, u32[]{:S(2)}) copy-start(f32[128,4,32]{0,2,1:T(8,128)} %param.10) | copy-start | bytes 196612
  52.8 32.6 %all-to-all-start = ((bf16[16,8,6,1024]{3,1,2,0:T(8,128)(2,1)}), bf16[16,8,6,1024]{3,1,2,0:T(8,128)(2,1)}, u32[]{:S(2)}, u32[]{:S(2)}) async-start(bf16[16,8,6,1024]{3,1,2,0:T(8,128)(2,1)} %copy.62), calls=%async_computation | async-start | bytes 3145728 | tf_op jit(solution)/shard_map/all_to_all | solution.py:41
  89.0 13.4 %all-to-all-start.1 = ((f32[16,8,6,128]{3,1,2,0:T(8,128)}), f32[16,8,6,128]{3,1,2,0:T(8,128)S(1)}, u32[]{:S(2)}, u32[]{:S(2)}) async-start(f32[16,8,6,128]{3,1,2,0:T(8,128)} %copy.64), calls=%async_computation.1 | async-start | bytes 786432 | tf_op jit(solution)/shard_map/all_to_all | solution.py:45
  92.6 196.5 %all-reduce.2.cloned.1.call-start = ((), (), s32[]{:S(2)}) async-start(), calls=%async_computation.6 | async-start | bytes 131072 | tf_op jit(solution)/shard_map/psum | solution.py:50
  250.4 243.1 %reduce-scatter.2.cloned.1.call-start = ((), (), s32[]{:S(2)}) async-start(), calls=%async_computation.7 | async-start | bytes 25165824 | tf_op jit(solution)/shard_map/reduce_scatter | solution.py:73
  446.7 13.7 %copy-start.2 = (bf16[128,4096]{1,0:T(8,128)(2,1)S(1)}, bf16[128,4096]{1,0:T(8,128)(2,1)}, u32[]{:S(2)}) copy-start(bf16[128,4096]{1,0:T(8,128)(2,1)} %param.7) | copy-start | bytes 3145732
  493.5 182.8 %collective-permute-start = (f32[2048,1024]{0,1:T(8,128)}, f32[2048,1024]{0,1:T(8,128)}, u32[]{:S(2)}, u32[]{:S(2)}) collective-permute-start(f32[2048,1024]{0,1:T(8,128)} %reduce-scatter.2.cloned.1.call-done), channel_id=1, source_target_pairs={{0,8},{8,0},{16,24},{24,16},{32,40},{40,32},{48,56},{56,48},{64,72... | collective-permute-start | bytes 25165832 | tf_op jit(solution)/shard_map/ppermute | solution.py:83
  688.2 183.5 %collective-permute-start.1 = (f32[2048,1024]{0,1:T(8,128)}, f32[2048,1024]{0,1:T(8,128)}, u32[]{:S(2)}, u32[]{:S(2)}) collective-permute-start(f32[2048,1024]{0,1:T(8,128)} %add.111), channel_id=1, source_target_pairs={{0,16},{8,24},{16,0},{24,8},{32,48},{40,56},{48,32},{56,40},{64,80... | collective-permute-start | bytes 25165832 | tf_op jit(solution)/shard_map/ppermute | solution.py:83
  883.5 181.1 %collective-permute-start.2 = (f32[2048,1024]{0,1:T(8,128)}, f32[2048,1024]{0,1:T(8,128)}, u32[]{:S(2)}, u32[]{:S(2)}) collective-permute-start(f32[2048,1024]{0,1:T(8,128)} %add.112), channel_id=1, source_target_pairs={{0,32},{8,40},{16,48},{24,56},{32,0},{40,8},{48,16},{56,24},{64,96... | collective-permute-start | bytes 25165832 | tf_op jit(solution)/shard_map/ppermute | solution.py:83
  1076.5 181.8 %collective-permute-start.3 = (f32[2048,1024]{0,1:T(8,128)}, f32[2048,1024]{0,1:T(8,128)}, u32[]{:S(2)}, u32[]{:S(2)}) collective-permute-start(f32[2048,1024]{0,1:T(8,128)} %add.113), channel_id=1, source_target_pairs={{0,64},{8,72},{16,80},{24,88},{32,96},{40,104},{48,112},{56,120},{... | collective-permute-start | bytes 25165832 | tf_op jit(solution)/shard_map/ppermute | solution.py:83
Sparse Core Ops, SparseCore 0:
  9.6 25.0 all-gather.1
  250.5 38.4 all-reduce.1
  468.6 24.7 reduce-scatter.1
